TPU v7x, 256 devices: a whole 4x4x8 slice. The times are simulated.
256 devices in a mesh: tests: 64 (over z, x, core), branches: 4 (over y).
Axes of the slice: x: 4, y: 4, z: 8, core: 2. Of those that a mesh axis runs over, the one named last changes fastest.
Arguments:
- select: float32 [1048576], P('tests'), may hold values from 1e-05 to 0.95
- tiles: float32 [16384, 128, 128], P(('tests', 'branches')), may hold values from 0.0001 to 0.9
- row_block: int32 [16384], P(('tests', 'branches')), may hold values from 0 to 127
- col_block: int32 [16384], P(('tests', 'branches')), may hold values from 0 to 2047, as said below
- counts: int32 [256], P(('tests', 'branches')), may hold values from 1 to 64, 10240 in all
- weights: float32 [1048576], P('branches'), may hold values from 1 to 16
Outputs:
- grad_tests: float32 [1048576], P('tests')
- tile_grads: float32 [16384, 128, 128], P(('tests', 'branches'))
- next_select: float32 [1048576], P('tests')
Inputs may be any that keep to these rules, and one draw needn't show every extreme that they name: counts[d] is the number of device d's slots, from its first, that hold tiles. Call col_block[s] // 32 the share of slot s. Of the 64 slots of one device at most 2 have one share; in every index of branches one share holds exactly 2 slots of every device there.
All inputs are finite; a program needn't handle non-finite values.
Results may differ from a plain program's by a relative error of at most 0.0003.
Values sent between devices are 32-bit elements; how exact they have to be, the bound alone decides.
A program may use at most 64 MiB of HBM per device.

v0:
```python
import jax
import jax.numpy as jnp
from jax import lax
from jax.sharding import PartitionSpec as P

STEPS = 2


ascent_rate = 0.0015
select_cap = 0.5


def tile_logs(blocks, tiles, rows, live):
    picked = blocks[rows]
    logs = jnp.sum(jnp.log1p(-picked[:, :, None] * tiles), axis=1)
    return jnp.where(live[:, None], logs, jnp.zeros_like(logs))


def tile_terms(blocks, slot_survive, tiles, rows, live):
    picked = blocks[rows]
    inverse = 1.0 / (1.0 - picked[:, :, None] * tiles)
    scaled = slot_survive[:, None, :] * inverse
    tests_part = jnp.sum(scaled * tiles, axis=2)
    tests_part = jnp.where(live[:, None], tests_part, jnp.zeros_like(tests_part))
    tile_part = scaled * picked[:, :, None]
    tile_part = jnp.where(live[:, None, None], tile_part, jnp.zeros_like(tile_part))
    return (tests_part, tile_part)


def body(select, tiles, row_block, col_block, counts, weights):
    width = tiles.shape[1]
    slots = tiles.shape[0]
    test_rows = select.shape[0] // width
    branch_rows = weights.shape[0] // width
    weight_rows = weights.reshape(branch_rows, width)
    limit = counts[0]
    current = select
    grad_tests = select
    tile_grads = tiles
    for step in range(STEPS):
        keep = step == STEPS - 1
        blocks = current.reshape(test_rows, width)
        live = jnp.arange(slots, dtype=jnp.int32) < limit
        slot_logs = tile_logs(blocks, tiles, row_block, live)
        partial_value = jnp.zeros((branch_rows, width), jnp.float32).at[col_block].add(slot_logs)
        summed = lax.psum(partial_value, "tests")
        slot_survive = (weight_rows * jnp.exp(summed))[col_block]
        empty_tests = jnp.zeros((test_rows, width), jnp.float32)
        live = jnp.arange(slots, dtype=jnp.int32) < limit
        tests_part, tile_part = tile_terms(blocks, slot_survive, tiles, row_block, live)
        tests_sum = empty_tests.at[row_block].add(tests_part)
        gradient = lax.psum(tests_sum, "branches").reshape(-1)
        if keep:
            grad_tests = gradient
            tile_grads = tile_part
        rate = ascent_rate * gradient
        current = current + (select_cap - current) * rate / (1.0 + rate)
    return (grad_tests, tile_grads, current)


def solution(mesh):
    return jax.shard_map(
        body,
        mesh=mesh,
        in_specs=(
            P("tests"),
            P(("tests", "branches"), None, None),
            P(("tests", "branches")),
            P(("tests", "branches")),
            P(("tests", "branches")),
            P("branches"),
        ),
        out_specs=(P("tests"), P(("tests", "branches"), None, None), P("tests")),
        check_vma=False,
    )
```

profile of v0, /device:TPU:1, one launch (start us, length us, event | category | flops | bytes accessed | tf_op | source)
XLA Modules:
  0.0 512.9 jit_solution(9038397558886190916)
XLA Ops:
  7.2 0.0 all-reduce.5.cloned.1.call-start
  8.0 0.7 compare_select_fusion.1
  8.6 0.7 compare_select_fusion
  9.3 1.4 gather_fusion
  10.7 3.3 log-plus-one_reduce_fusion.1
  14.1 1.9 scatter_custom_fusion
  15.9 0.0 all-reduce.5.cloned.1.call-update
  16.0 0.0 copy-start.1
  16.0 0.0 all-reduce.7.cloned.1.call-start
  16.0 188.5 %all-reduce.5.cloned.1.call-done = f32[2048,128]{1,0:T(8,128)} async-done(((f32[2048,128]{1,0:T(8,128)}), f32[2048,128]{1,0:T(8,128)}) %all-reduce.5.cloned.1.call-update) | async-done | bytes 1048592 | tf_op jit(solution)/shard_map/psum | solution.py:46
  204.5 1.4 bitcast_multiply_fusion.1
  205.9 0.6 gather_fusion.1
  206.5 4.5 multiply_reduce_fusion.1
  211.0 1.5 scatter_custom_fusion.1
  212.4 0.0 all-reduce.7.cloned.1.call-update
  212.4 0.0 all-reduce.9.cloned.1.call-start
  212.5 43.7 %all-reduce.7.cloned.1.call-done = f32[128,128]{1,0:T(8,128)} async-done(((f32[128,128]{1,0:T(8,128)}), f32[128,128]{1,0:T(8,128)}) %all-reduce.7.cloned.1.call-update) | async-done | bytes 65552 | tf_op jit(solution)/shard_map/psum | solution.py:52
  256.2 0.9 fusion.22
  257.1 0.6 gather_fusion.2
  257.7 3.3 log-plus-one_reduce_fusion
  261.1 1.9 scatter_custom_fusion.2
  262.9 0.0 all-reduce.9.cloned.1.call-update
  262.9 0.0 all-reduce.11.cloned.1.call-start
  263.0 187.3 %all-reduce.9.cloned.1.call-done = f32[2048,128]{1,0:T(8,128)} async-done(((f32[2048,128]{1,0:T(8,128)}), f32[2048,128]{1,0:T(8,128)}) %all-reduce.9.cloned.1.call-update) | async-done | bytes 1048592 | tf_op jit(solution)/shard_map/psum | solution.py:46
  450.3 1.4 bitcast_multiply_fusion
  451.7 0.6 gather_fusion.3
  452.3 5.9 %multiply_select_fusion = (f32[64,128,128]{2,1,0:T(8,128)}, f32[64,128]{1,0:T(8,128)S(1)}) fusion(f32[64,128,128]{2,1,0:T(8,128)} %param.7, f32[64,128]{1,0:T(8,128)S(1)} %gather_fusion.2, f32[64,128]{1,0:T(8,128)S(1)} %gather_fusion.3, pred[64]{0:T(512)(128)(4,1)S(1)} %iota_compare_fusion), kind=kLoop, calls=%fused_computation.8 | loop fusion | flops 8380416 | bytes 8486976 | tf_op jit(solution)/shard_map/jit(_where)/select_n | solution.py:26
  458.2 1.5 scatter_custom_fusion.3
  459.6 0.0 all-reduce.11.cloned.1.call-update
  459.7 43.8 %all-reduce.11.cloned.1.call-done = f32[16384]{0:T(1024)} async-done(((f32[16384]{0:T(1024)}), f32[16384]{0:T(1024)}) %all-reduce.11.cloned.1.call-update) | async-done | bytes 65552 | tf_op jit(solution)/shard_map/psum | solution.py:52
  503.4 1.5 divide_add_fusion
  504.9 1.5 copy.14
  (10 shorter events, 0.0 us)
Async XLA Ops:
  7.2 197.3 %copy-start = (f32[262144]{0:T(1024)S(1)}, f32[262144]{0:T(1024)}, u32[]{:S(2)}) copy-start(f32[262144]{0:T(1024)} %param.11) | copy-start | bytes 3145732
  7.2 197.3 %all-reduce.5.cloned.1.call-start = ((), (), s32[]{:S(2)}) async-start(), calls=%async_computation | async-start | bytes 2097152 | tf_op jit(solution)/shard_map/psum | solution.py:46
  16.0 240.3 %copy-start.1 = (f32[16384]{0:T(1024)S(1)}, f32[16384]{0:T(1024)}, u32[]{:S(2)}) copy-start(f32[16384]{0:T(1024)} %param.6) | copy-start | bytes 196612
  16.0 240.3 %all-reduce.7.cloned.1.call-start = ((), (), s32[]{:S(2)}) async-start(), calls=%async_computation.1 | async-start | bytes 131072 | tf_op jit(solution)/shard_map/psum | solution.py:52
  212.4 237.9 %all-reduce.9.cloned.1.call-start = ((), (), s32[]{:S(2)}) async-start(), calls=%async_computation.2 | async-start | bytes 2097152 | tf_op jit(solution)/shard_map/psum | solution.py:46
  262.9 240.5 %all-reduce.11.cloned.1.call-start = ((), (), s32[]{:S(2)}) async-start(), calls=%async_computation.3 | async-start | bytes 131072 | tf_op jit(solution)/shard_map/psum | solution.py:52
  452.3 51.1 %copy-start.2 = (f32[128,128]{1,0:T(8,128)S(1)}, f32[128,128]{1,0:T(8,128)}, u32[]{:S(2)}) copy-start(f32[128,128]{1,0:T(8,128)} %all-reduce.7.cloned.1.call-done) | copy-start | bytes 196612
Sparse Core Ops, SparseCore 0:
  16.1 188.3 all-reduce.4
  212.6 43.6 all-reduce.6
  263.1 187.2 all-reduce.8
  459.8 43.6 all-reduce.10
where the time goes:
time: 515 us; the launch traced here: 513 us
  waiting for transfers between devices  463 us (90%)
  other arithmetic  30.2 us (6%)
  between operations  14.6 us (3%)
    psum x2, waiting for transfers between devices, body(): summed = lax.psum(partial_value, 'tests')  376 us
    psum x2, waiting for transfers between devices, body(): gradient = lax.psum(tests_sum, 'branches').reshape(-1)  87.5 us
  transfers between devices with their start and end apart: 4, of which 4 were waited for; matrix products, arithmetic and copies ran while one was open for 0% of the time, Pallas kernels for 0%

commit v1 on v0

v1 whole, which is shorter than its diff:
```python
import functools

import jax
import jax.numpy as jnp
from jax import lax
from jax.experimental import pallas as pl
from jax.experimental.pallas import tpu as pltpu
from jax.sharding import PartitionSpec as P

MESH = pl.DeviceIdType.MESH
STEPS = 2
WIDTH = 128
GROUP = 8
CHAIN = 16
Z, X, C = 8, 4, 2

ascent_rate = 0.0015
select_cap = 0.5

exact = functools.partial(
    lax.dot_general,
    precision=lax.Precision.HIGHEST,
    preferred_element_type=jnp.float32,
)
ROWS = (((0,), (0,)), ((), ()))
PLAIN = (((1,), (0,)), ((), ()))


def iota(shape, axis):
    return lax.broadcasted_iota(jnp.int32, shape, axis)


def zigzag(k, size):
    half = (k + 1) // 2
    return size // 2 + half * (1 - 2 * (k % 2))


def ascend_kernel(
    n, share, slots, n_branches,
    select, rows, cols, counts, tiles_h, weights_h,
    grad_o, next_o, surv_o, cur_o,
    tiles_v, terms_v, meta_v, logs_v, surv_v, pick_v, route_v, hold_v, place_v, weights_v,
    a_send0, a_recv0, a_send1, a_recv1, b_send0, b_recv0, b_send1, b_recv1,
    g_send0, g_recv0, g_send1, g_recv1,
    tile_sem, local_sem, send_sem, recv_sem,
):
    t = lax.axis_index("tests")
    y = lax.axis_index("branches")
    z, x, c = t // (X * C), (t // C) % X, t % C
    groups = slots // GROUP

    def fetch(g):
        part = pl.ds(pl.multiple_of(g * GROUP, GROUP), GROUP)
        return pltpu.make_async_copy(tiles_h.at[part], tiles_v.at[part], tile_sem.at[g])

    for g in range(groups):
        fetch(g).start()
    own_weights = pltpu.make_async_copy(
        weights_h.at[pl.ds(pl.multiple_of(t * share, share), share)], weights_v, local_sem
    )
    own_weights.start()

    def ahead(i):
        dz, dx, dc = zigzag(i // (X * C), Z), zigzag((i // C) % X, X), 1 - i % C
        to = ((z + dz) % Z) * (X * C) + ((x + dx) % X) * C + (c + dc) % C
        back = ((z + Z - dz) % Z) * (X * C) + ((x + X - dx) % X) * C + (c + dc) % C
        return dz * (X * C) + dx * C + dc, to, back

    barrier = pltpu.get_barrier_semaphore()

    def greet(i, carry):
        _, to, _ = ahead(i)
        pl.semaphore_signal(barrier, inc=1, device_id=(to, y), device_id_type=MESH)
        return carry

    lax.fori_loop(0, n - 1, greet, 0)
    for d in range(1, n_branches):
        pl.semaphore_signal(
            barrier, inc=1, device_id=(t, (y + d) % n_branches), device_id_type=MESH
        )

    meta_v[...] = jnp.full_like(meta_v, -1)
    meta_v[0:1, 0:slots] = rows[...]
    meta_v[1:2, 0:slots] = cols[...]
    limit = counts[...]
    row_of, col_of = meta_v[0:1, :], meta_v[1:2, :]
    lane = iota((1, WIDTH), 1)
    live = lane < limit
    pick = (iota((WIDTH, WIDTH), 0) == row_of).astype(jnp.float32)
    pick_v[...] = pick
    owner, inside = col_of // share, col_of % share
    oz, ox, oc = owner // (X * C), (owner // C) % X, owner % C
    seat = ((oz + Z - z) % Z) * (X * C) + ((ox + X - x) % X) * C + (oc + C - c) % C
    seat = jnp.where(live, seat, n)
    takes = (iota((n, WIDTH), 0) == seat).astype(jnp.float32)
    earlier = (iota((WIDTH, WIDTH), 0) < iota((WIDTH, WIDTH), 1)).astype(jnp.float32)
    before = exact(takes, earlier, PLAIN)
    first = jnp.where(before < 0.5, takes, 0.0)
    second = takes - first
    route_v[0:n, :] = first
    route_v[n:2 * n, :] = second
    tag = (inside + 1).astype(jnp.float32)
    tag0 = jnp.sum(first * tag, axis=1, keepdims=True) - 1.0
    tag1 = jnp.sum(second * tag, axis=1, keepdims=True) - 1.0
    a_send0[:, 2, :] = jnp.where(iota((n, WIDTH), 1) < WIDTH // 2, tag0, tag1)

    logs_v[...] = jnp.zeros_like(logs_v)
    alive = iota((WIDTH, WIDTH), 0) < limit

    def send_all(src, dst, k, back):
        def one(i, carry):
            r, to, fro = ahead(i)
            pltpu.make_async_remote_copy(
                src_ref=src.at[r],
                dst_ref=dst.at[r],
                send_sem=send_sem.at[k],
                recv_sem=recv_sem.at[k],
                device_id=(fro if back else to, y),
                device_id_type=MESH,
            ).start()
            return carry

        lax.fori_loop(0, n - 1, one, 0)
        others = pl.ds(1, n - 1)
        return pltpu.make_async_remote_copy(
            src_ref=src.at[others],
            dst_ref=dst.at[others],
            send_sem=send_sem.at[k],
            recv_sem=recv_sem.at[k],
            device_id=(t, (y + 1) % n_branches),
            device_id_type=MESH,
        )

    a_bufs = ((a_send0, a_recv0), (a_send1, a_recv1))
    b_bufs = ((b_send0, b_recv0), (b_send1, b_recv1))
    g_bufs = ((g_send0, g_recv0), (g_send1, g_recv1))
    current = select[...]
    for step in range(STEPS):
        base = 3 * step
        a_send, a_recv = a_bufs[step]
        b_send, b_recv = b_bufs[step]
        g_send, g_recv = g_bufs[step]

        cur_o[...] = exact(current, pick_v[...], ROWS)

        def log_group(g, carry):
            if step == 0:
                fetch(g).wait()
            turned = pltpu.roll(cur_o[...], (WIDTH - GROUP * g) % WIDTH, 1)
            for i in range(GROUP):
                s = g * GROUP + i
                left = 1.0 - turned[:, i:i + 1] * tiles_v[s]
                left = left.reshape(CHAIN, WIDTH // CHAIN, WIDTH)
                part = left[0]
                for j in range(1, CHAIN):
                    part = part * left[j]
                logs_v[pl.ds(s, 1), :] = jnp.sum(jnp.log(part), axis=0, keepdims=True)
            return carry

        lax.fori_loop(0, groups, log_group, 0)
        logs = jnp.where(alive, logs_v[...], 0.0)
        packed = exact(route_v[...], logs, PLAIN)
        a_send[:, 0, :] = packed[0:n]
        a_send[:, 1, :] = packed[n:2 * n]
        if step == 0:
            pl.semaphore_wait(barrier, n - 1 + n_branches - 1)
        a_wait = send_all(a_send, a_recv, base, False)
        a_recv[0] = a_send[0]

        def term_group(g, carry):
            turned = pltpu.roll(cur_o[...], (WIDTH - GROUP * g) % WIDTH, 1)
            for i in range(GROUP):
                s = g * GROUP + i
                tile = tiles_v[s]
                terms_v[s] = tile / (1.0 - turned[:, i:i + 1] * tile)
            return carry

        lax.fori_loop(0, groups, term_group, 0)
        if step == 0:
            own_weights.wait()
        a_wait.wait_recv()

        if step == 0:
            tags = a_recv[:, 2, :]
            hold_v[...] = (
                tags == (iota((n, WIDTH), 1) % (WIDTH // 2)).astype(jnp.float32)
            ).astype(jnp.float32)
        hold = hold_v[...]
        both = jnp.concatenate([a_recv[:, 0, :], a_recv[:, 1, :]], axis=1)
        sums = exact(hold, both, ROWS)
        half = WIDTH // 2
        summed = sums[0:share, 0:WIDTH] + sums[half:half + share, WIDTH:]
        survival = weights_v[...] * jnp.exp(summed)
        gap = jnp.zeros((half - share, WIDTH), jnp.float32)
        none = jnp.zeros((half, WIDTH), jnp.float32)
        spread = jnp.concatenate(
            [
                jnp.concatenate([survival, gap, none], axis=0),
                jnp.concatenate([none, survival, gap], axis=0),
            ],
            axis=1,
        )
        replies = exact(hold, spread, PLAIN)
        b_send[:, 0, :] = replies[:, 0:WIDTH]
        b_send[:, 1, :] = replies[:, WIDTH:]
        b_wait = send_all(b_send, b_recv, base + 1, True)
        b_recv[0] = b_send[0]
        b_wait.wait_recv()
        got = jnp.concatenate([b_recv[:, 0, :], b_recv[:, 1, :]], axis=0)
        surv_v[...] = exact(route_v[...], got, ROWS)

        def grad_group(g, acc):
            for i in range(GROUP):
                s = g * GROUP + i
                col = jnp.sum(terms_v[s] * surv_v[pl.ds(s, 1), :], axis=1, keepdims=True)
                acc = jnp.where(iota((WIDTH, WIDTH), 1) == s, col, acc)
            return acc

        acc = lax.fori_loop(0, groups, grad_group, jnp.zeros((WIDTH, WIDTH), jnp.float32))
        parts = acc.T
        g_send[0:slots, :] = parts[0:slots]
        if step == 0:
            g_send[slots:slots + 8, :] = jnp.broadcast_to(row_of.astype(jnp.float32), (8, WIDTH))
        for d in (2, 1, 3):
            pltpu.make_async_remote_copy(
                src_ref=g_send,
                dst_ref=g_recv.at[y],
                send_sem=send_sem.at[base + 2],
                recv_sem=recv_sem.at[base + 2],
                device_id=(t, (y + d) % n_branches),
                device_id_type=MESH,
            ).start()
        g_recv[y] = g_send[...]
        g_wait = pltpu.make_async_remote_copy(
            src_ref=g_recv.at[pl.ds(0, n_branches - 1)],
            dst_ref=g_recv.at[pl.ds(0, n_branches - 1)],
            send_sem=send_sem.at[base + 2],
            recv_sem=recv_sem.at[base + 2],
            device_id=(t, (y + 1) % n_branches),
            device_id_type=MESH,
        )
        g_wait.wait_recv()
        if step == 0:
            for q in range(0, n_branches, 2):
                low = g_recv[q, slots:slots + 1, :]
                high = pltpu.roll(g_recv[q + 1, slots:slots + 8, :], WIDTH // 2, 1)[0:1]
                names = jnp.where(lane < slots, low, high)
                place_v[:, q * slots:(q + 2) * slots] = (
                    iota((WIDTH, WIDTH), 0).astype(jnp.float32) == names
                ).astype(jnp.float32)
        pieces = jnp.concatenate([g_recv[q, 0:slots, :] for q in range(n_branches)], axis=0)
        gradient = exact(place_v[...], pieces, PLAIN)
        rate = ascent_rate * gradient
        current = current + (select_cap - current) * rate / (1.0 + rate)
        a_wait.wait_send()
        b_wait.wait_send()
        g_wait.wait_send()
    grad_o[...] = gradient
    next_o[...] = current
    surv_o[...] = surv_v[0:slots, :]


def tiles_kernel(surv, cur, tiles, out):
    g = pl.program_id(0)
    turned = pltpu.roll(cur[...], (WIDTH - GROUP * g) % WIDTH, 1)
    for i in range(GROUP):
        picked = turned[:, i:i + 1]
        out[i] = surv[i:i + 1, :] * picked / (1.0 - picked * tiles[i])


def body(n, n_branches, select, tiles, row_block, col_block, counts, weights):
    slots = tiles.shape[0]
    test_rows = select.shape[0] // WIDTH
    branch_rows = weights.shape[0] // WIDTH
    share = branch_rows // n
    f32 = jnp.float32
    vmem = pl.BlockSpec(memory_space=pltpu.VMEM)
    hbm = pl.BlockSpec(memory_space=pl.ANY)
    square = jax.ShapeDtypeStruct((WIDTH, WIDTH), f32)
    message = lambda k: pltpu.VMEM((n, k, WIDTH), f32)
    grad_tests, next_select, surv, cur = pl.pallas_call(
        functools.partial(ascend_kernel, n, share, slots, n_branches),
        out_shape=(square, square, jax.ShapeDtypeStruct((slots, WIDTH), f32), square),
        in_specs=[vmem, vmem, vmem, vmem, hbm, hbm],
        out_specs=[vmem] * 4,
        scratch_shapes=[
            pltpu.VMEM(tiles.shape, f32),
            pltpu.VMEM(tiles.shape, f32),
            pltpu.VMEM((8, WIDTH), jnp.int32),
            pltpu.VMEM((WIDTH, WIDTH), f32),
            pltpu.VMEM((WIDTH, WIDTH), f32),
            pltpu.VMEM((WIDTH, WIDTH), f32),
            pltpu.VMEM((2 * n, WIDTH), f32),
            pltpu.VMEM((n, WIDTH), f32),
            pltpu.VMEM((WIDTH, n_branches * slots), f32),
            pltpu.VMEM((share, WIDTH), f32),
            message(3), message(3), message(2), message(2),
            message(2), message(2), message(2), message(2),
            pltpu.VMEM((slots + 8, WIDTH), f32),
            pltpu.VMEM((n_branches, slots + 8, WIDTH), f32),
            pltpu.VMEM((slots, WIDTH), f32),
            pltpu.VMEM((n_branches, slots, WIDTH), f32),
            pltpu.SemaphoreType.DMA((slots // GROUP,)),
            pltpu.SemaphoreType.DMA,
            pltpu.SemaphoreType.DMA((3 * STEPS,)),
            pltpu.SemaphoreType.DMA((3 * STEPS,)),
        ],
        compiler_params=pltpu.CompilerParams(
            collective_id=0, has_side_effects=True, vmem_limit_bytes=32 << 20
        ),
        name="ascend",
    )(
        select.reshape(test_rows, WIDTH),
        row_block.reshape(1, slots),
        col_block.reshape(1, slots),
        counts.reshape(1, 1),
        tiles,
        weights.reshape(branch_rows, WIDTH),
    )
    block = pl.BlockSpec((GROUP, WIDTH, WIDTH), lambda g: (g, 0, 0))
    tile_grads = pl.pallas_call(
        tiles_kernel,
        grid=(slots // GROUP,),
        out_shape=jax.ShapeDtypeStruct(tiles.shape, f32),
        in_specs=[
            pl.BlockSpec((GROUP, WIDTH), lambda g: (g, 0)),
            pl.BlockSpec((WIDTH, WIDTH), lambda g: (0, 0)),
            block,
        ],
        out_specs=block,
        name="tile_terms",
    )(surv, cur, tiles)
    return grad_tests.reshape(-1), tile_grads, next_select.reshape(-1)


def solution(mesh):
    n, n_branches = mesh.shape["tests"], mesh.shape["branches"]
    return jax.shard_map(
        functools.partial(body, n, n_branches),
        mesh=mesh,
        in_specs=(
            P("tests"),
            P(("tests", "branches"), None, None),
            P(("tests", "branches")),
            P(("tests", "branches")),
            P(("tests", "branches")),
            P("branches"),
        ),
        out_specs=(P("tests"), P(("tests", "branches"), None, None), P("tests")),
        check_vma=False,
    )
```

time: 515 us -> 73.7 us (0.14)
  waiting for transfers between devices: 463 us -> 0 us
  Pallas kernels: 0 us -> 63.9 us
  other arithmetic: 30.2 us -> 0 us
  between operations: 14.6 us -> 1.31 us
    psum x4 -> x0, waiting for transfers between devices: 463 us -> none  [the longest x2 376 us: body(): summed = lax.psum(partial_value, 'tests')]
    pallas_call x0 -> x2, Pallas kernels: none -> 63.9 us  [the longest x1 56.4 us: body(): pl.pallas_call(functools.partial(ascend_kernel, n, share, slots, n_branch...]
    reduce_sum x3 -> x0, other arithmetic: 11.2 us -> none  [the longest x2 6.68 us: tile_logs(): logs = jnp.sum(jnp.log1p(-picked[:, :, None] * tiles), axis=1)]
    select_n x3 -> x0, other arithmetic: 7.2 us -> none  [the longest x1 5.88 us: tile_terms(): jnp.where(live[:, None, None], tile_part, jnp.zeros_like(tile_part))]
    scatter-add x4 -> x0, other arithmetic: 6.65 us -> none  [the longest x2 3.73 us: body(): jnp.zeros((branch_rows, width), jnp.float32).at[col_block].add(slot_logs)]
    unnamed x7 -> x16, local copies, waits for them, and re-layouts: 1.49 us -> 8.06 us
  transfers between devices with their start and end apart: 4 -> 0, of which waited for: 4 -> 0; matrix products, arithmetic and copies ran while one was open for 0% -> 0% of each run, Pallas kernels for 0% -> 0%
where the time goes in v1:
time: 73.7 us; the launch traced here: 73.3 us
  Pallas kernels  63.9 us (87%)
  local copies, waits for them, and re-layouts  8.06 us (11%)
  between operations  1.31 us (2%)
    pallas_call x1, Pallas kernels, body(): pl.pallas_call(functools.partial(ascend_kernel, n, share, slots, n_branch...  56.4 us
    unnamed x16, local copies, waits for them, and re-layouts  8.06 us
    pallas_call x1, Pallas kernels, body(): pl.pallas_call(tiles_kernel, grid=(slots // GROUP,), out_shape=jax.ShapeD...  7.57 us

profile of v1, /device:TPU:1, one launch (start us, length us, event | category | flops | bytes accessed | tf_op | source)
XLA Modules:
  0.0 73.3 jit_solution(5171974676276682211)
XLA Ops:
  1.3 0.0 copy-start
  1.3 2.2 %copy-done = f32[64,128,128]{2,1,0:T(8,128)S(1)} copy-done((f32[64,128,128]{2,1,0:T(8,128)S(1)}, f32[64,128,128]{2,1,0:T(8,128)}, u32[]{:S(2)}) %copy-start) | copy-done | bytes 4194328
  3.5 0.0 copy-start.1
  3.5 1.2 %copy-done.1 = f32[262144]{0:T(1024)S(1)} copy-done((f32[262144]{0:T(1024)S(1)}, f32[262144]{0:T(1024)}, u32[]{:S(2)}) %copy-start.1) | copy-done | bytes 1048600
  4.7 0.0 copy-start.2
  4.7 0.8 %copy-done.2 = f32[16384]{0:T(1024)S(1)} copy-done((f32[16384]{0:T(1024)S(1)}, f32[16384]{0:T(1024)}, u32[]{:S(2)}) %copy-start.2) | copy-done | bytes 65560
  5.5 0.0 copy-start.5
  5.5 0.7 copy-done.5
  6.2 0.0 copy-start.6
  6.2 0.7 copy-done.6
  6.8 56.4 %ascend.1 = (f32[128,128]{1,0:T(8,128)S(1)}, f32[128,128]{1,0:T(8,128)S(1)}, f32[64,128]{1,0:T(8,128)S(1)}, f32[128,128]{1,0:T(8,128)S(1)}) custom-call(f32[128,128]{1,0:T(8,128)S(1)} %bitcast.9, s32[1,64]{1,0:T(1,128)S(1)} %bitcast.12, s32[1,64]{1,0:T(1,128)S(1)} %bitcast.13, s32[1,1]{1,0:T(1,128)} %bitcast.7.counts, f32[64,128,128]{2,1,0:T(8,128)S(1)} %copy-done, ...), custom_call_target="tpu_custom_call" | custom-call | tf_op jit(solution)/shard_map/ascend/pallas_call | solution.py:281
  63.2 0.0 copy-start.3
  63.2 0.6 copy-done.3
  63.9 0.0 copy-start.4
  63.9 0.6 copy-done.4
  64.5 7.6 %tile_terms.1 = f32[64,128,128]{2,1,0:T(8,128)} custom-call(f32[64,128]{1,0:T(8,128)} %copy-done.4, f32[128,128]{1,0:T(8,128)} %copy-done.3, f32[64,128,128]{2,1,0:T(8,128)} %tiles.1), custom_call_target="tpu_custom_call" | custom-call | tf_op jit(solution)/shard_map/tile_terms/pallas_call | solution.py:321
  72.0 0.6 copy.12
  72.7 0.6 copy.13
Async XLA Ops:
  1.3 2.2 %copy-start = (f32[64,128,128]{2,1,0:T(8,128)S(1)}, f32[64,128,128]{2,1,0:T(8,128)}, u32[]{:S(2)}) copy-start(f32[64,128,128]{2,1,0:T(8,128)} %tiles.1) | copy-start | bytes 12582916
  3.5 1.2 %copy-start.1 = (f32[262144]{0:T(1024)S(1)}, f32[262144]{0:T(1024)}, u32[]{:S(2)}) copy-start(f32[262144]{0:T(1024)} %param.11) | copy-start | bytes 3145732
  4.7 0.8 %copy-start.2 = (f32[16384]{0:T(1024)S(1)}, f32[16384]{0:T(1024)}, u32[]{:S(2)}) copy-start(f32[16384]{0:T(1024)} %param.6) | copy-start | bytes 196612
  5.5 0.7 copy-start.5
  6.2 0.7 copy-start.6
  63.2 0.6 copy-start.3
  63.9 0.6 copy-start.4

commit v2 on v1

--- a/solution.py
+++ b/solution.py
@@ -37,12 +37,12 @@
 
 def ascend_kernel(
     n, share, slots, n_branches,
-    select, rows, cols, counts, tiles_h, weights_h,
-    grad_o, next_o, surv_o, cur_o,
-    tiles_v, terms_v, meta_v, logs_v, surv_v, pick_v, route_v, hold_v, place_v, weights_v,
+    select_h, rows_h, cols_h, counts_h, tiles_h, weights_h,
+    grad_o, next_o, tile_o,
+    select, rows, cols, counts, cur_v, tiles_v, terms_v, meta_v, logs_v, surv_v, pick_v, route_v, hold_v, place_v, weights_v,
     a_send0, a_recv0, a_send1, a_recv1, b_send0, b_recv0, b_send1, b_recv1,
     g_send0, g_recv0, g_send1, g_recv1,
-    tile_sem, local_sem, send_sem, recv_sem,
+    tile_sem, local_sem, small_sem, send_sem, recv_sem,
 ):
     t = lax.axis_index("tests")
     y = lax.axis_index("branches")
@@ -53,6 +53,14 @@
         part = pl.ds(pl.multiple_of(g * GROUP, GROUP), GROUP)
         return pltpu.make_async_copy(tiles_h.at[part], tiles_v.at[part], tile_sem.at[g])
 
+    smalls = [
+        pltpu.make_async_copy(src, dst, small_sem.at[i])
+        for i, (src, dst) in enumerate(
+            ((select_h, select), (rows_h, rows), (cols_h, cols), (counts_h, counts))
+        )
+    ]
+    for copy in smalls:
+        copy.start()
     for g in range(groups):
         fetch(g).start()
     own_weights = pltpu.make_async_copy(
@@ -79,6 +87,8 @@
             barrier, inc=1, device_id=(t, (y + d) % n_branches), device_id_type=MESH
         )
 
+    for copy in smalls:
+        copy.wait()
     meta_v[...] = jnp.full_like(meta_v, -1)
     meta_v[0:1, 0:slots] = rows[...]
     meta_v[1:2, 0:slots] = cols[...]
@@ -137,16 +147,17 @@
     current = select[...]
     for step in range(STEPS):
         base = 3 * step
+        last = step == STEPS - 1
         a_send, a_recv = a_bufs[step]
         b_send, b_recv = b_bufs[step]
         g_send, g_recv = g_bufs[step]
 
-        cur_o[...] = exact(current, pick_v[...], ROWS)
+        cur_v[...] = exact(current, pick_v[...], ROWS)
 
         def log_group(g, carry):
             if step == 0:
                 fetch(g).wait()
-            turned = pltpu.roll(cur_o[...], (WIDTH - GROUP * g) % WIDTH, 1)
+            turned = pltpu.roll(cur_v[...], (WIDTH - GROUP * g) % WIDTH, 1)
             for i in range(GROUP):
                 s = g * GROUP + i
                 left = 1.0 - turned[:, i:i + 1] * tiles_v[s]
@@ -168,11 +179,15 @@
         a_recv[0] = a_send[0]
 
         def term_group(g, carry):
-            turned = pltpu.roll(cur_o[...], (WIDTH - GROUP * g) % WIDTH, 1)
+            turned = pltpu.roll(cur_v[...], (WIDTH - GROUP * g) % WIDTH, 1)
             for i in range(GROUP):
                 s = g * GROUP + i
                 tile = tiles_v[s]
-                terms_v[s] = tile / (1.0 - turned[:, i:i + 1] * tile)
+                picked = turned[:, i:i + 1]
+                inverse = 1.0 / (1.0 - picked * tile)
+                terms_v[s] = tile * inverse
+                if last:
+                    tile_o[s] = picked * inverse
             return carry
 
         lax.fori_loop(0, groups, term_group, 0)
@@ -207,7 +222,7 @@
         b_recv[0] = b_send[0]
         b_wait.wait_recv()
         got = jnp.concatenate([b_recv[:, 0, :], b_recv[:, 1, :]], axis=0)
-        surv_v[...] = exact(route_v[...], got, ROWS)
+        surv_v[...] = jnp.where(alive, exact(route_v[...], got, ROWS), 0.0)
 
         def grad_group(g, acc):
             for i in range(GROUP):
@@ -239,6 +254,15 @@
             device_id=(t, (y + 1) % n_branches),
             device_id_type=MESH,
         )
+        if last:
+
+            def tile_group(g, carry):
+                for i in range(GROUP):
+                    s = g * GROUP + i
+                    tile_o[s] = tile_o[s] * surv_v[pl.ds(s, 1), :]
+                return carry
+
+            lax.fori_loop(0, groups, tile_group, 0)
         g_wait.wait_recv()
         if step == 0:
             for q in range(0, n_branches, 2):
@@ -257,15 +281,17 @@
         g_wait.wait_send()
     grad_o[...] = gradient
     next_o[...] = current
-    surv_o[...] = surv_v[0:slots, :]
-
-
-def tiles_kernel(surv, cur, tiles, out):
-    g = pl.program_id(0)
-    turned = pltpu.roll(cur[...], (WIDTH - GROUP * g) % WIDTH, 1)
-    for i in range(GROUP):
-        picked = turned[:, i:i + 1]
-        out[i] = surv[i:i + 1, :] * picked / (1.0 - picked * tiles[i])
+
+
+def store_kernel(count, *refs):
+    copies = [
+        pltpu.make_async_copy(refs[i], refs[count + i], refs[2 * count].at[i])
+        for i in range(count)
+    ]
+    for copy in copies:
+        copy.start()
+    for copy in copies:
+        copy.wait()
 
 
 def body(n, n_branches, select, tiles, row_block, col_block, counts, weights):
@@ -275,15 +301,23 @@
     share = branch_rows // n
     f32 = jnp.float32
     vmem = pl.BlockSpec(memory_space=pltpu.VMEM)
-    hbm = pl.BlockSpec(memory_space=pl.ANY)
+    hbm = pl.BlockSpec(memory_space=pltpu.HBM)
     square = jax.ShapeDtypeStruct((WIDTH, WIDTH), f32)
+    shapes = (square, square, jax.ShapeDtypeStruct(tiles.shape, f32))
+    held = tuple(pltpu.VMEM(a.shape, f32) for a in shapes)
+    stay = lambda a: pltpu.with_memory_space_constraint(a, pltpu.HBM)
     message = lambda k: pltpu.VMEM((n, k, WIDTH), f32)
-    grad_tests, next_select, surv, cur = pl.pallas_call(
+    results = pl.pallas_call(
         functools.partial(ascend_kernel, n, share, slots, n_branches),
-        out_shape=(square, square, jax.ShapeDtypeStruct((slots, WIDTH), f32), square),
-        in_specs=[vmem, vmem, vmem, vmem, hbm, hbm],
-        out_specs=[vmem] * 4,
+        out_shape=held,
+        in_specs=[hbm] * 6,
+        out_specs=[vmem] * 3,
         scratch_shapes=[
+            pltpu.VMEM((test_rows, WIDTH), f32),
+            pltpu.VMEM((1, slots), jnp.int32),
+            pltpu.VMEM((1, slots), jnp.int32),
+            pltpu.VMEM((1, 1), jnp.int32),
+            pltpu.VMEM((WIDTH, WIDTH), f32),
             pltpu.VMEM(tiles.shape, f32),
             pltpu.VMEM(tiles.shape, f32),
             pltpu.VMEM((8, WIDTH), jnp.int32),
@@ -302,11 +336,12 @@
             pltpu.VMEM((n_branches, slots, WIDTH), f32),
             pltpu.SemaphoreType.DMA((slots // GROUP,)),
             pltpu.SemaphoreType.DMA,
+            pltpu.SemaphoreType.DMA((4,)),
             pltpu.SemaphoreType.DMA((3 * STEPS,)),
             pltpu.SemaphoreType.DMA((3 * STEPS,)),
         ],
         compiler_params=pltpu.CompilerParams(
-            collective_id=0, has_side_effects=True, vmem_limit_bytes=32 << 20
+            collective_id=0, has_side_effects=True, vmem_limit_bytes=59 << 20
         ),
         name="ascend",
     )(
@@ -317,19 +352,15 @@
         tiles,
         weights.reshape(branch_rows, WIDTH),
     )
-    block = pl.BlockSpec((GROUP, WIDTH, WIDTH), lambda g: (g, 0, 0))
-    tile_grads = pl.pallas_call(
-        tiles_kernel,
-        grid=(slots // GROUP,),
-        out_shape=jax.ShapeDtypeStruct(tiles.shape, f32),
-        in_specs=[
-            pl.BlockSpec((GROUP, WIDTH), lambda g: (g, 0)),
-            pl.BlockSpec((WIDTH, WIDTH), lambda g: (0, 0)),
-            block,
-        ],
-        out_specs=block,
-        name="tile_terms",
-    )(surv, cur, tiles)
+    grad_tests, next_select, tile_grads = pl.pallas_call(
+        functools.partial(store_kernel, len(shapes)),
+        out_shape=shapes,
+        in_specs=[vmem] * len(shapes),
+        out_specs=[hbm] * len(shapes),
+        scratch_shapes=[pltpu.SemaphoreType.DMA((len(shapes),))],
+        compiler_params=pltpu.CompilerParams(vmem_limit_bytes=1 << 20),
+        name="store",
+    )(*results)
     return grad_tests.reshape(-1), tile_grads, next_select.reshape(-1)
 
 

time: 73.7 us -> 59.7 us (0.81)
  local copies, waits for them, and re-layouts: 8.06 us -> 0 us
  Pallas kernels: 63.9 us -> 58.4 us
    unnamed x16 -> x0, local copies, waits for them, and re-layouts: 8.06 us -> none
    pallas_call x1, Pallas kernels: 7.57 us -> 2.08 us  [body(): pl.pallas_call(functools.partial(store_kernel, len(shapes)), out_shape=sh...]
where the time goes in v2:
time: 59.7 us
  Pallas kernels  58.4 us (98%)
  between operations  1.29 us (2%)
    pallas_call x1, Pallas kernels, body(): pl.pallas_call(functools.partial(ascend_kernel, n, share, slots, n_branch...  56.3 us
    pallas_call x1, Pallas kernels, body(): pl.pallas_call(functools.partial(store_kernel, len(shapes)), out_shape=sh...  2.08 us

profile of v2, /device:TPU:1, one launch (start us, length us, event | category | flops | bytes accessed | tf_op | source)
XLA Modules:
  0.0 59.7 jit_solution(11634092871380813353)
XLA Ops:
  1.3 56.3 %ascend.1 = (f32[128,128]{1,0:T(8,128)S(1)}, f32[128,128]{1,0:T(8,128)S(1)}, f32[64,128,128]{2,1,0:T(8,128)S(1)}) custom-call(f32[128,128]{1,0:T(8,128)} %bitcast.9, s32[1,64]{1,0:T(1,128)} %bitcast.10, s32[1,64]{1,0:T(1,128)} %bitcast.11, s32[1,1]{1,0:T(1,128)} %bitcast.7.counts_h, f32[64,128,128]{2,1,0:T(8,128)} %tiles_h.1, f32[2048,128]{1,0:T(8,128)} %bitcast.8), custom_call_target="tpu_custom_call" | custom-call | tf_op jit(solution)/shard_map/ascend/pallas_call | solution.py:310
  57.6 2.1 %store.1 = (f32[128,128]{1,0:T(8,128)}, f32[128,128]{1,0:T(8,128)}, f32[64,128,128]{2,1,0:T(8,128)}) custom-call(f32[128,128]{1,0:T(8,128)S(1)} %get-tuple-element.9.refs_0_, f32[128,128]{1,0:T(8,128)S(1)} %get-tuple-element.10.refs_1_, f32[64,128,128]{2,1,0:T(8,128)S(1)} %get-tuple-element.11.refs_2_), custom_call_target="tpu_custom_call" | custom-call | tf_op jit(solution)/shard_map/store/pallas_call | solution.py:355

commit v3 on v2

--- a/solution.py
+++ b/solution.py
@@ -9,6 +9,8 @@
 
 MESH = pl.DeviceIdType.MESH
 STEPS = 2
+HALVES = 2
+PIECES = 8
 WIDTH = 128
 GROUP = 8
 CHAIN = 16
@@ -17,13 +19,25 @@
 ascent_rate = 0.0015
 select_cap = 0.5
 
-exact = functools.partial(
-    lax.dot_general,
-    precision=lax.Precision.HIGHEST,
-    preferred_element_type=jnp.float32,
-)
 ROWS = (((0,), (0,)), ((), ()))
 PLAIN = (((1,), (0,)), ((), ()))
+
+
+def thirds(x):
+    high = x.astype(jnp.bfloat16)
+    rest = x - high.astype(jnp.float32)
+    middle = rest.astype(jnp.bfloat16)
+    low = (rest - middle.astype(jnp.float32)).astype(jnp.bfloat16)
+    return low, middle, high
+
+
+def dot(a, b, dims):
+    return lax.dot_general(a, b, dims, preferred_element_type=jnp.float32)
+
+
+def select_by(mask, x, dims):
+    low, middle, high = (dot(mask.astype(jnp.bfloat16), part, dims) for part in thirds(x))
+    return low + middle + high
 
 
 def iota(shape, axis):
@@ -61,31 +75,31 @@
     ]
     for copy in smalls:
         copy.start()
+    def ahead(i):
+        dz, dx, dc = zigzag(i // (X * C), Z), zigzag((i // C) % X, X), 1 - i % C
+        to = ((z + dz) % Z) * (X * C) + ((x + dx) % X) * C + (c + dc) % C
+        back = ((z + Z - dz) % Z) * (X * C) + ((x + X - dx) % X) * C + (c + dc) % C
+        return dz * (X * C) + dx * C + dc, to, back
+
+    barrier = pltpu.get_barrier_semaphore()
+
+    def greet(i, carry):
+        _, to, _ = ahead(i)
+        pl.semaphore_signal(barrier, inc=1, device_id=(to, y), device_id_type=MESH)
+        return carry
+
+    lax.fori_loop(0, n - 1, greet, 0)
+    for d in range(1, n_branches):
+        pl.semaphore_signal(
+            barrier, inc=1, device_id=(t, (y + d) % n_branches), device_id_type=MESH
+        )
+
     for g in range(groups):
         fetch(g).start()
     own_weights = pltpu.make_async_copy(
         weights_h.at[pl.ds(pl.multiple_of(t * share, share), share)], weights_v, local_sem
     )
     own_weights.start()
-
-    def ahead(i):
-        dz, dx, dc = zigzag(i // (X * C), Z), zigzag((i // C) % X, X), 1 - i % C
-        to = ((z + dz) % Z) * (X * C) + ((x + dx) % X) * C + (c + dc) % C
-        back = ((z + Z - dz) % Z) * (X * C) + ((x + X - dx) % X) * C + (c + dc) % C
-        return dz * (X * C) + dx * C + dc, to, back
-
-    barrier = pltpu.get_barrier_semaphore()
-
-    def greet(i, carry):
-        _, to, _ = ahead(i)
-        pl.semaphore_signal(barrier, inc=1, device_id=(to, y), device_id_type=MESH)
-        return carry
-
-    lax.fori_loop(0, n - 1, greet, 0)
-    for d in range(1, n_branches):
-        pl.semaphore_signal(
-            barrier, inc=1, device_id=(t, (y + d) % n_branches), device_id_type=MESH
-        )
 
     for copy in smalls:
         copy.wait()
@@ -104,7 +118,7 @@
     seat = jnp.where(live, seat, n)
     takes = (iota((n, WIDTH), 0) == seat).astype(jnp.float32)
     earlier = (iota((WIDTH, WIDTH), 0) < iota((WIDTH, WIDTH), 1)).astype(jnp.float32)
-    before = exact(takes, earlier, PLAIN)
+    before = dot(takes.astype(jnp.bfloat16), earlier.astype(jnp.bfloat16), PLAIN)
     first = jnp.where(before < 0.5, takes, 0.0)
     second = takes - first
     route_v[0:n, :] = first
@@ -113,6 +127,8 @@
     tag0 = jnp.sum(first * tag, axis=1, keepdims=True) - 1.0
     tag1 = jnp.sum(second * tag, axis=1, keepdims=True) - 1.0
     a_send0[:, 2, :] = jnp.where(iota((n, WIDTH), 1) < WIDTH // 2, tag0, tag1)
+
+    g_send0[slots:slots + 8, :] = jnp.broadcast_to(row_of.astype(jnp.float32), (8, WIDTH))
 
     logs_v[...] = jnp.zeros_like(logs_v)
     alive = iota((WIDTH, WIDTH), 0) < limit
@@ -152,7 +168,9 @@
         b_send, b_recv = b_bufs[step]
         g_send, g_recv = g_bufs[step]
 
-        cur_v[...] = exact(current, pick_v[...], ROWS)
+        picks = pick_v[...].astype(jnp.bfloat16)
+        low, middle, high = (dot(part, picks, ROWS) for part in thirds(current))
+        cur_v[...] = low + middle + high
 
         def log_group(g, carry):
             if step == 0:
@@ -170,13 +188,28 @@
 
         lax.fori_loop(0, groups, log_group, 0)
         logs = jnp.where(alive, logs_v[...], 0.0)
-        packed = exact(route_v[...], logs, PLAIN)
+        packed = select_by(route_v[...], logs, PLAIN)
         a_send[:, 0, :] = packed[0:n]
         a_send[:, 1, :] = packed[n:2 * n]
         if step == 0:
             pl.semaphore_wait(barrier, n - 1 + n_branches - 1)
         a_wait = send_all(a_send, a_recv, base, False)
         a_recv[0] = a_send[0]
+
+        def send_rows(start, count):
+            part = pl.ds(start, count)
+            for d in (2, 1, 3):
+                pltpu.make_async_remote_copy(
+                    src_ref=g_send.at[part],
+                    dst_ref=g_recv.at[y, part],
+                    send_sem=send_sem.at[base + 2],
+                    recv_sem=recv_sem.at[base + 2],
+                    device_id=(t, (y + d) % n_branches),
+                    device_id_type=MESH,
+                ).start()
+
+        if step == 0:
+            send_rows(slots, 8)
 
         def term_group(g, carry):
             turned = pltpu.roll(cur_v[...], (WIDTH - GROUP * g) % WIDTH, 1)
@@ -202,7 +235,7 @@
             ).astype(jnp.float32)
         hold = hold_v[...]
         both = jnp.concatenate([a_recv[:, 0, :], a_recv[:, 1, :]], axis=1)
-        sums = exact(hold, both, ROWS)
+        sums = select_by(hold, both, ROWS)
         half = WIDTH // 2
         summed = sums[0:share, 0:WIDTH] + sums[half:half + share, WIDTH:]
         survival = weights_v[...] * jnp.exp(summed)
@@ -215,14 +248,14 @@
             ],
             axis=1,
         )
-        replies = exact(hold, spread, PLAIN)
+        replies = select_by(hold, spread, PLAIN)
         b_send[:, 0, :] = replies[:, 0:WIDTH]
         b_send[:, 1, :] = replies[:, WIDTH:]
         b_wait = send_all(b_send, b_recv, base + 1, True)
         b_recv[0] = b_send[0]
         b_wait.wait_recv()
         got = jnp.concatenate([b_recv[:, 0, :], b_recv[:, 1, :]], axis=0)
-        surv_v[...] = jnp.where(alive, exact(route_v[...], got, ROWS), 0.0)
+        surv_v[...] = jnp.where(alive, select_by(route_v[...], got, ROWS), 0.0)
 
         def grad_group(g, acc):
             for i in range(GROUP):
@@ -231,20 +264,16 @@
                 acc = jnp.where(iota((WIDTH, WIDTH), 1) == s, col, acc)
             return acc
 
-        acc = lax.fori_loop(0, groups, grad_group, jnp.zeros((WIDTH, WIDTH), jnp.float32))
-        parts = acc.T
-        g_send[0:slots, :] = parts[0:slots]
-        if step == 0:
-            g_send[slots:slots + 8, :] = jnp.broadcast_to(row_of.astype(jnp.float32), (8, WIDTH))
-        for d in (2, 1, 3):
-            pltpu.make_async_remote_copy(
-                src_ref=g_send,
-                dst_ref=g_recv.at[y],
-                send_sem=send_sem.at[base + 2],
-                recv_sem=recv_sem.at[base + 2],
-                device_id=(t, (y + d) % n_branches),
-                device_id_type=MESH,
-            ).start()
+        for h in range(HALVES):
+            acc = lax.fori_loop(
+                h * groups // HALVES,
+                (h + 1) * groups // HALVES,
+                grad_group,
+                jnp.zeros((WIDTH, WIDTH), jnp.float32),
+            )
+            start, count = h * slots // HALVES, slots // HALVES
+            g_send[start:start + count, :] = acc.T[start:start + count]
+            send_rows(start, count)
         g_recv[y] = g_send[...]
         g_wait = pltpu.make_async_remote_copy(
             src_ref=g_recv.at[pl.ds(0, n_branches - 1)],
@@ -273,7 +302,7 @@
                     iota((WIDTH, WIDTH), 0).astype(jnp.float32) == names
                 ).astype(jnp.float32)
         pieces = jnp.concatenate([g_recv[q, 0:slots, :] for q in range(n_branches)], axis=0)
-        gradient = exact(place_v[...], pieces, PLAIN)
+        gradient = select_by(place_v[...], pieces, PLAIN)
         rate = ascent_rate * gradient
         current = current + (select_cap - current) * rate / (1.0 + rate)
         a_wait.wait_send()
@@ -284,10 +313,17 @@
 
 
 def store_kernel(count, *refs):
-    copies = [
-        pltpu.make_async_copy(refs[i], refs[count + i], refs[2 * count].at[i])
-        for i in range(count)
-    ]
+    sems = refs[2 * count]
+    copies = []
+    for i in reversed(range(count)):
+        src, dst = refs[i], refs[count + i]
+        rows = src.shape[0]
+        size = rows // PIECES if len(src.shape) == 3 else rows
+        for start in range(0, rows, size):
+            part = pl.ds(start, size)
+            copies.append(
+                pltpu.make_async_copy(src.at[part], dst.at[part], sems.at[len(copies)])
+            )
     for copy in copies:
         copy.start()
     for copy in copies:
@@ -357,7 +393,7 @@
         out_shape=shapes,
         in_specs=[vmem] * len(shapes),
         out_specs=[hbm] * len(shapes),
-        scratch_shapes=[pltpu.SemaphoreType.DMA((len(shapes),))],
+        scratch_shapes=[pltpu.SemaphoreType.DMA((len(shapes) - 1 + PIECES,))],
         compiler_params=pltpu.CompilerParams(vmem_limit_bytes=1 << 20),
         name="store",
     )(*results)

time: 59.7 us -> 59.2 us (level)
  Pallas kernels: 58.4 us -> 57.8 us
    pallas_call x1, Pallas kernels: 56.3 us -> 55.7 us  [body(): pl.pallas_call(functools.partial(ascend_kernel, n, share, slots, n_branch...]
where the time goes in v3:
time: 59.2 us; the launch traced here: 59.1 us
  Pallas kernels  57.8 us (98%)
  between operations  1.29 us (2%)
    pallas_call x1, Pallas kernels, body(): pl.pallas_call(functools.partial(ascend_kernel, n, share, slots, n_branch...  55.7 us
    pallas_call x1, Pallas kernels, body(): pl.pallas_call(functools.partial(store_kernel, len(shapes)), out_shape=sh...  2.12 us

profile of v3, /device:TPU:1, one launch (start us, length us, event | category | flops | bytes accessed | tf_op | source)
XLA Modules:
  0.0 59.1 jit_solution(13852750633425815063)
XLA Ops:
  1.3 55.7 %ascend.1 = (f32[128,128]{1,0:T(8,128)S(1)}, f32[128,128]{1,0:T(8,128)S(1)}, f32[64,128,128]{2,1,0:T(8,128)S(1)}) custom-call(f32[128,128]{1,0:T(8,128)} %bitcast.9, s32[1,64]{1,0:T(1,128)} %bitcast.10, s32[1,64]{1,0:T(1,128)} %bitcast.11, s32[1,1]{1,0:T(1,128)} %bitcast.7.counts_h, f32[64,128,128]{2,1,0:T(8,128)} %tiles_h.1, f32[2048,128]{1,0:T(8,128)} %bitcast.8), custom_call_target="tpu_custom_call" | custom-call | tf_op jit(solution)/shard_map/ascend/pallas_call | solution.py:346
  57.0 2.1 %store.1 = (f32[128,128]{1,0:T(8,128)}, f32[128,128]{1,0:T(8,128)}, f32[64,128,128]{2,1,0:T(8,128)}) custom-call(f32[128,128]{1,0:T(8,128)S(1)} %get-tuple-element.9.refs_0_, f32[128,128]{1,0:T(8,128)S(1)} %get-tuple-element.10.refs_1_, f32[64,128,128]{2,1,0:T(8,128)S(1)} %get-tuple-element.11.refs_2_), custom_call_target="tpu_custom_call" | custom-call | tf_op jit(solution)/shard_map/store/pallas_call | solution.py:391
